TPU v7x, 32 devices: a whole 2x2x4 slice. The times are simulated.
32 devices in a mesh: row: 2 (over x), col: 4 (over y, core), layer: 4 (over z).
Axes of the slice: x: 2, y: 2, z: 4, core: 2. Of those that a mesh axis runs over, the one named last changes fastest.
Arguments:
- source_matrix_strip: bfloat16 [4096, 512], P('row', 'col')
- target_matrix_strip: bfloat16 [512, 8192], P('row', ('col', 'layer'))
- stored_tile_flag: int32 [32, 4], P('row', 'col'), may hold values from 0 to 1
- target_place_tile_index: int32 [32, 32], P('row', ('col', 'layer')), may hold values from 0 to 3, as said below
- retained_target_flag: int32 [32, 32], P('row', ('col', 'layer')), may hold values 0 or 1
Outputs:
- clustered: bfloat16 [4096, 4096], P(('row', 'layer'), 'col')
Inputs may be any that keep to these rules, and one draw needn't show every extreme that they name: `target_place_tile_index`: within each block row, the 2 slots of one column tile name distinct column blocks.
All inputs are finite; a program needn't handle non-finite values. No bound on the sum of `retained_target_flag` on one device may be relied on, other than what follows from the above.
Results may differ from a plain program's by a relative error of at most 0.0012.
Values may be sent and summed in bfloat16 or wider, within the bound.
No kernel may reach another device: no remote copies, remote signals or barrier semaphores. Data moves between devices by JAX's collectives and lax.ppermute only.
A program may use at most 64 MiB of HBM per device.

v0:
```python
import jax
import jax.numpy as jnp
from jax import lax
from jax.sharding import PartitionSpec as P

BS = 128
COLB = 4
KOL = 2


def matrix_squaring_step(walk_matrix_result, target_place_tile_index, retained_target_flag):
    block_rows = walk_matrix_result.shape[0] // BS
    product_blocks = walk_matrix_result.reshape(block_rows, BS, COLB, BS)
    block_selector = (
        target_place_tile_index[:, :, None] == jnp.arange(COLB, dtype=jnp.int32)[None, None, :]
    ).astype(jnp.float32)
    picked = jnp.einsum(
        "rsc,rick->rsik", block_selector, product_blocks, precision=lax.Precision.HIGHEST
    )
    retain_weight = retained_target_flag.astype(jnp.float32)
    raised_power_blocks = picked * picked * retain_weight[:, :, None, None]
    row_sums = jnp.sum(raised_power_blocks, axis=2)
    partial_column_sums = jnp.einsum(
        "rsc,rsk->ck", block_selector, row_sums, precision=lax.Precision.HIGHEST
    )
    return (block_selector, raised_power_blocks, partial_column_sums)


def normalize_blocks(block_selector, raised_power_blocks, column_sums, total_rows):
    column_mean = column_sums / jnp.float32(total_rows)
    denominator = (
        jnp.einsum("rsc,ck->rsk", block_selector, column_mean, precision=lax.Precision.HIGHEST)
        + 1e-06
    )
    normalized = (raised_power_blocks / denominator[:, :, None, :]).astype(jnp.bfloat16)
    block_rows = raised_power_blocks.shape[0]
    return jnp.transpose(normalized, (0, 2, 1, 3)).reshape(block_rows * BS, KOL * BS)


def shards(
    source_matrix_strip,
    target_matrix_strip,
    stored_tile_flag,
    target_place_tile_index,
    retained_target_flag,
):
    local_rows = source_matrix_strip.shape[0]
    expanded = jnp.repeat(jnp.repeat(stored_tile_flag, BS, axis=0), BS, axis=1)
    masked = source_matrix_strip * expanded.astype(jnp.bfloat16)
    right_whole = lax.all_gather(target_matrix_strip, "row", axis=0, tiled=True)
    total_rows = local_rows * lax.axis_size("row")
    walk_matrix_result = jnp.dot(
        lax.all_gather(masked, "col", axis=1, tiled=True),
        right_whole,
        preferred_element_type=jnp.float32,
    )
    block_selector, raised_power_blocks, partial_column_sums = matrix_squaring_step(
        walk_matrix_result, target_place_tile_index, retained_target_flag
    )
    column_sums = lax.psum(partial_column_sums, "row")
    arranged = normalize_blocks(block_selector, raised_power_blocks, column_sums, total_rows)
    return lax.all_to_all(arranged, "layer", split_axis=0, concat_axis=1, tiled=True)


def solution(mesh):
    placed = (
        P("row", "col"),
        P("row", ("col", "layer")),
        P("row", "col"),
        P("row", ("col", "layer")),
        P("row", ("col", "layer")),
    )
    return jax.shard_map(
        shards, mesh=mesh, in_specs=placed, out_specs=P(("row", "layer"), "col"), check_vma=False
    )
```

profile of v0, /device:TPU:0, one launch (start us, length us, event | category | flops | bytes accessed | tf_op | source)
XLA Modules:
  0.0 96.9 jit_solution(11177682488823599812)
XLA Ops:
  6.5 0.0 all-gather.2.cloned.1.call-start
  6.5 0.7 convert_bitcast_fusion
  7.2 0.1 broadcast_bitcast_fusion
  7.3 2.2 %broadcast_multiply_fusion = bf16[2048,128]{1,0:T(8,128)(2,1)} fusion(bf16[2048,128]{1,0:T(8,128)(2,1)} %param.5, bf16[2048]{0:T(1024)(128)(2,1)S(1)} %broadcast_bitcast_fusion), kind=kLoop, calls=%fused_computation.5 | loop fusion | flops 262144 | bytes 1052672 | tf_op jit(solution)/shard_map/mul | solution.py:49
  9.4 0.0 all-gather.2.cloned.1.call-update
  9.5 0.7 fusion.2
  10.2 0.1 copy.10
  10.3 0.7 convert_element_type.25
  11.0 0.1 copy.7
  11.0 10.2 %all_gather.7 = bf16[512,512]{1,0:T(8,128)(2,1)S(1)} all-gather(bf16[256,512]{1,0:T(8,128)(2,1)} %param.6), channel_id=1, replica_groups=mesh['row'=2,'col'=4,'layer'=4] {'row'}, dimensions={0}, use_global_device_ids=true | all-gather | bytes 786432 | tf_op jit(solution)/shard_map/all_gather | solution.py:50
  21.2 14.0 %all-gather.2.cloned.1.call-done = bf16[2048,512]{1,0:T(8,128)(2,1)} async-done(((bf16[2048,128]{1,0:T(8,128)(2,1)}), bf16[2048,512]{1,0:T(8,128)(2,1)}) %all-gather.2.cloned.1.call-update) | async-done | bytes 2097168 | tf_op jit(solution)/shard_map/all_gather | solution.py:53
  35.2 4.8 %fusion.10 = f32[2048,512]{1,0:T(8,128)} fusion(bf16[2048,512]{1,0:T(8,128)(2,1)} %all-gather.2.cloned.1.call-done, bf16[512,512]{1,0:T(8,128)(2,1)S(1)} %all_gather.7), kind=kOutput, calls=%fused_computation.18 | convolution fusion | flops 1073741824 | bytes 6815744 | tf_op jit(solution)/shard_map/dot_general | solution.py:52
  39.9 5.2 %reshape.22 = f32[16,128,4,128]{3,2,1,0:T(4,128)} reshape(f32[2048,512]{1,0:T(8,128)} %fusion.10) | data formatting | bytes 8388608 | tf_op jit(solution)/shard_map/reshape | solution.py:13
  45.2 0.0 copy-start
  45.2 7.3 %fusion.9 = (f32[16,2,128]{2,1,0:T(2,128)S(1)}, f32[16,2,128,128]{3,1,2,0:T(2,128)S(1)}) fusion(f32[16,2]{1,0:T(8,128)S(1)} %copy.7, pred[16,2,4,1]{2,1,3,0:T(4,128)(4,1)S(1)} %copy.10, f32[16,128,4,128]{3,2,1,0:T(4,128)} %reshape.22), kind=kOutput, calls=%fused_computation.17 | convolution fusion | flops 26734592 | bytes 6308096 | tf_op jit(solution)/shard_map/rsc,rick->rsik/dot_general | solution.py:17
  52.5 0.0 copy-done
  52.5 0.2 convolution_bitcast_fusion
  52.7 4.9 %psum.7 = f32[4,128]{1,0:T(4,128)S(1)} all-reduce(f32[4,128]{1,0:T(4,128)S(1)} %convolution_bitcast_fusion), channel_id=1, replica_groups=mesh['row'=2,'col'=4,'layer'=4] {'row'}, use_global_device_ids=true, to_apply=%region_1.0 | all-reduce | flops 512 | bytes 4096 | tf_op jit(solution)/shard_map/psum | solution.py:60
  57.6 0.2 convolution_add_fusion
  57.9 0.9 fusion
  58.8 0.7 all_to_all.14
  59.5 29.4 %all_to_all.19 = bf16[4,512,256]{2,1,0:T(8,128)(2,1)S(1)} all-to-all(bf16[4,512,256]{2,1,0:T(8,128)(2,1)S(1)} %all_to_all.14), channel_id=1, replica_groups=mesh['row'=2,'col'=4,'layer'=4] {'layer'}, dimensions={0} | all-to-all | bytes 2097152 | tf_op jit(solution)/shard_map/all_to_all | solution.py:62
  88.9 1.1 %copy.14 = bf16[4,64,8,256]{3,2,0,1:T(8,128)(2,1)} copy(bf16[4,64,8,256]{3,2,1,0:T(8,128)(2,1)S(1)} %bitcast.20) | data formatting | bytes 2097152 | tf_op jit(solution)/shard_map/all_to_all | solution.py:62
  (1 shorter events, 0.0 us)
Async XLA Ops:
  6.5 28.6 %all-gather.2.cloned.1.call-start = ((), (), s32[]{:S(2)}) async-start(), calls=%async_computation.1 | async-start | bytes 2621440 | tf_op jit(solution)/shard_map/all_gather | solution.py:53
  45.2 7.3 %copy-start = (s32[16,2]{0,1:T(2,128)S(1)}, s32[16,2]{0,1:T(2,128)}, u32[]{:S(2)}) copy-start(s32[16,2]{0,1:T(2,128)} %param.8) | copy-start | bytes 388
Sparse Core Ops, SparseCore 0:
  9.6 25.5 all-gather.1
where the time goes:
time: 97.3 us; the launch traced here: 96.9 us
  blocking collectives  44.5 us (46%)
  waiting for transfers between devices  14 us (14%)
  between operations  13.4 us (14%)
  matrix products  12.5 us (13%)
  local copies, waits for them, and re-layouts  7.34 us (8%)
  other arithmetic  5.11 us (5%)
    all_to_all x1, blocking collectives, shards(): lax.all_to_all(arranged, 'layer', split_axis=0, concat_axis=1, tiled=True)  29.4 us
    all_gather x1, waiting for transfers between devices, shards(): lax.all_gather(masked, 'col', axis=1, tiled=True)  14 us
    all_gather x1, blocking collectives, shards(): right_whole = lax.all_gather(target_matrix_strip, 'row', axis=0, tiled=True)  10.2 us
    dot_general x1, matrix products, matrix_squaring_step(): jnp.einsum('rsc,rick->rsik', block_selector, product_blocks, precision=la...  7.34 us
    reshape x1, local copies, waits for them, and re-layouts, matrix_squaring_step(): product_blocks = walk_matrix_result.reshape(block_rows, BS, COLB, BS)  5.23 us
    psum x1, blocking collectives, shards(): column_sums = lax.psum(partial_column_sums, 'row')  4.93 us
    dot_general x1, matrix products, shards(): jnp.dot(lax.all_gather(masked, 'col', axis=1, tiled=True), right_whole, p...  4.76 us
    mul x1, other arithmetic, shards(): masked = source_matrix_strip * expanded.astype(jnp.bfloat16)  2.18 us
  transfers between devices with their start and end apart: 1, of which 1 were waited for; matrix products, arithmetic and copies ran while one was open for 2% of the time, Pallas kernels for 0%

commit v1 on v0

--- a/solution.py
+++ b/solution.py
@@ -6,6 +6,29 @@
 BS = 128
 COLB = 4
 KOL = 2
+
+
+def _note_roads(arr, dim_k):
+    arr = jnp.moveaxis(arr, 0, dim_k)
+    extra = arr.shape
+    return arr.reshape(*extra[:dim_k], extra[dim_k] * extra[dim_k + 1], *extra[dim_k + 2 :])
+
+
+def show_screen_up(work_x, which_axis, axis_no):
+    devs = lax.axis_size(which_axis)
+    tray = [(hop_no, (hop_no + 1) % devs) for hop_no in range(devs)]
+    r_now, h_now = ([], [])
+    crops = [(j0, to_i) for to_i, j0 in tray]
+    for w in tuple(range(devs - 1)):
+        if w % 2 == 0:
+            r_now.append(lax.ppermute(r_now[-1] if r_now else work_x, which_axis, perm=tray))
+        else:
+            h_now.append(lax.ppermute(h_now[-1] if h_now else work_x, which_axis, crops))
+    tile_out = jnp.stack([*r_now[::-1], work_x, *h_now])
+    mixed_arr = lax.axis_index(which_axis)
+    t_next = mixed_arr - len(r_now)
+    tile_out = tile_out[(jnp.arange(devs) - t_next) % devs]
+    return _note_roads(tile_out, axis_no)
 
 
 def matrix_squaring_step(walk_matrix_result, target_place_tile_index, retained_target_flag):
@@ -50,9 +73,7 @@
     right_whole = lax.all_gather(target_matrix_strip, "row", axis=0, tiled=True)
     total_rows = local_rows * lax.axis_size("row")
     walk_matrix_result = jnp.dot(
-        lax.all_gather(masked, "col", axis=1, tiled=True),
-        right_whole,
-        preferred_element_type=jnp.float32,
+        show_screen_up(masked, "col", 1), right_whole, preferred_element_type=jnp.float32
     )
     block_selector, raised_power_blocks, partial_column_sums = matrix_squaring_step(
         walk_matrix_result, target_place_tile_index, retained_target_flag

time: 97.3 us -> 81.5 us (0.84)
  between operations: 13.4 us -> 0.13 us
  waiting for transfers between devices: 14 us -> 6.15 us
  local copies, waits for them, and re-layouts: 7.34 us -> 11.8 us
  starting transfers between devices: 0.01 us -> 4.38 us
  matrix products: 12.5 us -> 8.16 us
    all_gather x1 -> x0, waiting for transfers between devices: 14 us -> none  [shards(): lax.all_gather(masked, 'col', axis=1, tiled=True)]
    dot_general x0 -> x3, local copies, waits for them, and re-layouts: none -> 7.52 us  [shards(): jnp.dot(show_screen_up(masked, 'col', 1), right_whole, preferred_element_...]
    ppermute x0 -> x3, waiting for transfers between devices: none -> 6.15 us  [the longest x2 6.14 us: show_screen_up(): lax.ppermute(r_now[-1] if r_now else work_x, which_axis, perm=tray)]
    reshape x1 -> x0, local copies, waits for them, and re-layouts: 5.23 us -> none  [matrix_squaring_step(): product_blocks = walk_matrix_result.reshape(block_rows, BS, COLB, BS)]
    ppermute x0 -> x3, starting transfers between devices: none -> 4.38 us  [the longest x2 2.36 us: show_screen_up(): lax.ppermute(r_now[-1] if r_now else work_x, which_axis, perm=tray)]
    dot_general x1, matrix products: 4.76 us -> 1.25 us  [shards(): jnp.dot(show_screen_up(masked, 'col', 1), right_whole, preferred_element_...]
    gather x0 -> x1, local copies, waits for them, and re-layouts: none -> 2.16 us  [show_screen_up(): tile_out = tile_out[(jnp.arange(devs) - t_next) % devs]]
    another operation x0 -> x2, other arithmetic: none -> 1.79 us  [show_screen_up(): tile_out = jnp.stack([*r_now[::-1], work_x, *h_now])]
  transfers between devices with their start and end apart: 1 -> 3, of which waited for: 1 -> 1; matrix products, arithmetic and copies ran while one was open for 2% -> 2% of each run, Pallas kernels for 0% -> 0%
where the time goes in v1:
time: 81.5 us; the launch traced here: 81.2 us
  blocking collectives  45.1 us (55%)
  local copies, waits for them, and re-layouts  11.8 us (14%)
  matrix products  8.16 us (10%)
  waiting for transfers between devices  6.15 us (8%)
  other arithmetic  5.52 us (7%)
  starting transfers between devices  4.38 us (5%)
    all_to_all x1, blocking collectives, shards(): lax.all_to_all(arranged, 'layer', split_axis=0, concat_axis=1, tiled=True)  30.1 us
    all_gather x1, blocking collectives, shards(): right_whole = lax.all_gather(target_matrix_strip, 'row', axis=0, tiled=True)  9.71 us
    dot_general x3, local copies, waits for them, and re-layouts, shards(): jnp.dot(show_screen_up(masked, 'col', 1), right_whole, preferred_element_...  7.52 us
    dot_general x1, matrix products, matrix_squaring_step(): jnp.einsum('rsc,rick->rsik', block_selector, product_blocks, precision=la...  6.51 us
    ppermute x2, waiting for transfers between devices, show_screen_up(): lax.ppermute(r_now[-1] if r_now else work_x, which_axis, perm=tray)  6.14 us
    psum x1, blocking collectives, shards(): column_sums = lax.psum(partial_column_sums, 'row')  5.28 us
    ppermute x2, starting transfers between devices, show_screen_up(): lax.ppermute(r_now[-1] if r_now else work_x, which_axis, perm=tray)  2.36 us
    gather x1, local copies, waits for them, and re-layouts, show_screen_up(): tile_out = tile_out[(jnp.arange(devs) - t_next) % devs]  2.16 us
  transfers between devices with their start and end apart: 3, of which 1 were waited for; matrix products, arithmetic and copies ran while one was open for 2% of the time, Pallas kernels for 0%

profile of v1, /device:TPU:0, one launch (start us, length us, event | category | flops | bytes accessed | tf_op | source)
XLA Modules:
  0.0 81.2 jit_solution(6879871850827203873)
XLA Ops:
  0.0 0.7 convert_bitcast_fusion
  0.8 1.4 %broadcast_multiply_fusion = bf16[2048,128]{1,0:T(8,128)(2,1)S(1)} fusion(bf16[2048,128]{1,0:T(8,128)(2,1)} %param.5, bf16[2048]{0:T(1024)(128)(2,1)S(1)} %broadcast_bitcast_fusion), kind=kLoop, calls=%fused_computation.11 | loop fusion | flops 262144 | bytes 1052672 | tf_op jit(solution)/shard_map/mul | solution.py:72
  2.2 0.5 collective-permute-start
  2.7 2.0 %collective-permute-start.2 = (bf16[2048,128]{1,0:T(8,128)(2,1)S(1)}, bf16[2048,128]{1,0:T(8,128)(2,1)}, u32[]{:S(2)}, u32[]{:S(2)}) collective-permute-start(bf16[2048,128]{1,0:T(8,128)(2,1)S(1)} %broadcast_multiply_fusion), channel_id=1, source_target_pairs={{4,0},{8,4},{12,8},{0,12},{5,1},{9,5},{13,9},{1,13},{6,2},{10,6},{... | collective-permute-start | bytes 1572872 | tf_op jit(solution)/shard_map/ppermute | solution.py:26
  4.7 9.7 %all_gather.3 = bf16[512,512]{1,0:T(8,128)(2,1)S(1)} all-gather(bf16[256,512]{1,0:T(8,128)(2,1)} %param.6), channel_id=1, replica_groups=mesh['row'=2,'col'=4,'layer'=4] {'row'}, dimensions={0}, use_global_device_ids=true | all-gather | bytes 786432 | tf_op jit(solution)/shard_map/all_gather | solution.py:73
  14.4 0.7 fusion.8
  15.1 1.9 %collective-permute-start.1 = (bf16[2048,128]{1,0:T(8,128)(2,1)S(1)}, bf16[2048,128]{1,0:T(8,128)(2,1)}, u32[]{:S(2)}, u32[]{:S(2)}) collective-permute-start(bf16[2048,128]{1,0:T(8,128)(2,1)S(1)} %collective-permute-done), channel_id=1, source_target_pairs={{0,4},{4,8},{8,12},{12,0},{1,5},{5,9},{9,13},{13,1},{2,6},{6,10},{... | collective-permute-start | bytes 1572872 | tf_op jit(solution)/shard_map/ppermute | solution.py:24
  17.0 0.1 reshape.82
  17.2 0.1 copy.18
  17.3 0.3 fusion.20
  17.7 6.1 %collective-permute-done.1 = bf16[2048,128]{1,0:T(8,128)(2,1)} collective-permute-done((bf16[2048,128]{1,0:T(8,128)(2,1)S(1)}, bf16[2048,128]{1,0:T(8,128)(2,1)}, u32[]{:S(2)}, u32[]{:S(2)}) %collective-permute-start.1) | collective-permute-done | bytes 524320 | tf_op jit(solution)/shard_map/ppermute | solution.py:24
  23.8 1.5 %pad_maximum_fusion = bf16[4,2048,128]{2,1,0:T(8,128)(2,1)S(1)} fusion(bf16[1,2048,128]{2,1,0:T(8,128)(2,1)} %bitcast.6, bf16[1,2048,128]{2,1,0:T(8,128)(2,1)S(1)} %fusion.20, bf16[1,2048,128]{2,1,0:T(8,128)(2,1)S(1)} %bitcast.32, bf16[1,2048,128]{2,1,0:T(8,128)(2,1)} %bitcast.3), kind=kLoop, calls=%fused_computation.3 | loop fusion | flops 3145728 | bytes 4194304 | tf_op jit(solution)/shard_map/stack | solution.py:27
  25.3 2.2 %gather_fusion = bf16[4,2048,128]{2,1,0:T(8,128)(2,1)} fusion(bf16[4,2048,128]{2,1,0:T(8,128)(2,1)S(1)} %pad_maximum_fusion, s32[1024]{0:T(1024)S(1)} %pad_clamp_fusion), kind=kCustom, calls=%fused_computation | custom fusion | bytes 4194320 | tf_op jit(solution)/shard_map/gather | solution.py:30
  27.5 4.7 %copy.22 = bf16[2048,4,128]{2,1,0:T(4,128)(2,1)} copy(bf16[2048,4,128]{2,0,1:T(8,128)(2,1)} %bitcast.29) | data formatting | bytes 4194304 | tf_op jit(solution)/shard_map/dot_general | solution.py:75
  32.1 2.7 %reshape.87 = bf16[16,128,512,1]{2,1,3,0:T(8,128)(2,1)S(1)} reshape(bf16[2048,4,128]{2,1,0:T(4,128)(2,1)} %copy.22) | data formatting | bytes 4194304 | tf_op jit(solution)/shard_map/dot_general | solution.py:75
  34.9 1.3 %fusion.5 = f32[16,128,4,128]{3,1,2,0:T(8,128)S(1)} fusion(bf16[16,128,512,1]{2,1,3,0:T(8,128)(2,1)S(1)} %reshape.87, bf16[4,128,512,1]{1,0,2,3:T(4,128)(2,1)S(1)} %reshape.82), kind=kOutput, calls=%fused_computation.9 | convolution fusion | flops 1073741824 | bytes 6815744 | tf_op jit(solution)/shard_map/dot_general | solution.py:75
  36.1 6.5 %fusion.17 = (f32[16,2,128]{2,1,0:T(2,128)S(1)}, f32[16,2,128,128]{3,1,2,0:T(2,128)S(1)}) fusion(f32[16,2]{1,0:T(8,128)S(1)} %copy.12, pred[16,2,4,1]{2,1,3,0:T(4,128)(4,1)S(1)} %copy.18, f32[16,128,4,128]{3,1,2,0:T(8,128)S(1)} %fusion.5), kind=kOutput, calls=%fused_computation.30 | convolution fusion | flops 26734592 | bytes 6308096 | tf_op jit(solution)/shard_map/rsc,rick->rsik/dot_general | solution.py:40
  42.7 0.2 convolution_bitcast_fusion
  42.9 5.3 %psum.7 = f32[4,128]{1,0:T(4,128)S(1)} all-reduce(f32[4,128]{1,0:T(4,128)S(1)} %convolution_bitcast_fusion), channel_id=1, replica_groups=mesh['row'=2,'col'=4,'layer'=4] {'row'}, use_global_device_ids=true, to_apply=%region_1.2 | all-reduce | flops 512 | bytes 4096 | tf_op jit(solution)/shard_map/psum | solution.py:81
  48.1 0.2 convolution_add_fusion
  48.4 0.9 %fusion.4 = bf16[16,128,2,128]{3,2,1,0:T(2,128)(2,1)S(1)} fusion(f32[16,2,128,128]{3,1,2,0:T(2,128)S(1)} %get-tuple-element.6, f32[16,2,128]{2,1,0:T(2,128)S(1)} %copy.13), kind=kLoop, calls=%fused_computation.8 | loop fusion | flops 1048576 | bytes 3162112 | tf_op jit(solution)/shard_map/convert_element_type | solution.py:58
  49.3 0.7 all_to_all.14
  50.0 30.1 %all_to_all.19 = bf16[4,512,256]{2,1,0:T(8,128)(2,1)S(1)} all-to-all(bf16[4,512,256]{2,1,0:T(8,128)(2,1)S(1)} %all_to_all.14), channel_id=1, replica_groups=mesh['row'=2,'col'=4,'layer'=4] {'layer'}, dimensions={0} | all-to-all | bytes 2097152 | tf_op jit(solution)/shard_map/all_to_all | solution.py:83
  80.1 1.1 %copy.24 = bf16[4,64,8,256]{3,2,0,1:T(8,128)(2,1)} copy(bf16[4,64,8,256]{3,2,1,0:T(8,128)(2,1)S(1)} %bitcast.30) | data formatting | bytes 2097152 | tf_op jit(solution)/shard_map/all_to_all | solution.py:83
  (14 shorter events, 0.2 us)
Async XLA Ops:
  0.0 17.3 %copy-start = (bf16[2048,128]{1,0:T(8,128)(2,1)S(1)}, bf16[2048,128]{1,0:T(8,128)(2,1)}, u32[]{:S(2)}) copy-start(bf16[2048,128]{1,0:T(8,128)(2,1)} %param.5) | copy-start | bytes 1572868
  0.0 17.1 %copy-start.2 = (s32[16,2]{0,1:T(2,128)S(1)}, s32[16,2]{0,1:T(2,128)}, u32[]{:S(2)}) copy-start(s32[16,2]{0,1:T(2,128)} %param.9) | copy-start | bytes 388
  2.2 12.9 %collective-permute-start = (bf16[2048,128]{1,0:T(8,128)(2,1)S(1)}, bf16[2048,128]{1,0:T(8,128)(2,1)S(1)}, u32[]{:S(2)}, u32[]{:S(2)}) collective-permute-start(bf16[2048,128]{1,0:T(8,128)(2,1)S(1)} %broadcast_multiply_fusion), channel_id=1, source_target_pairs={{0,4},{4,8},{8,12},{12,0},{1,5},{5,9},{9,13},{13,1},{2,6},{6,10},{... | collective-permute-start | bytes 1572872 | tf_op jit(solution)/shard_map/ppermute | solution.py:24
  2.7 15.0 %collective-permute-start.2 = (bf16[2048,128]{1,0:T(8,128)(2,1)S(1)}, bf16[2048,128]{1,0:T(8,128)(2,1)}, u32[]{:S(2)}, u32[]{:S(2)}) collective-permute-start(bf16[2048,128]{1,0:T(8,128)(2,1)S(1)} %broadcast_multiply_fusion), channel_id=1, source_target_pairs={{4,0},{8,4},{12,8},{0,12},{5,1},{9,5},{13,9},{1,13},{6,2},{10,6},{... | collective-permute-start | bytes 1572872 | tf_op jit(solution)/shard_map/ppermute | solution.py:26
  15.1 8.7 %collective-permute-start.1 = (bf16[2048,128]{1,0:T(8,128)(2,1)S(1)}, bf16[2048,128]{1,0:T(8,128)(2,1)}, u32[]{:S(2)}, u32[]{:S(2)}) collective-permute-start(bf16[2048,128]{1,0:T(8,128)(2,1)S(1)} %collective-permute-done), channel_id=1, source_target_pairs={{0,4},{4,8},{8,12},{12,0},{1,5},{5,9},{9,13},{13,1},{2,6},{6,10},{... | collective-permute-start | bytes 1572872 | tf_op jit(solution)/shard_map/ppermute | solution.py:24
  36.1 6.5 %copy-start.1 = (s32[16,2]{0,1:T(2,128)S(1)}, s32[16,2]{0,1:T(2,128)}, u32[]{:S(2)}) copy-start(s32[16,2]{0,1:T(2,128)} %param.8) | copy-start | bytes 388
